TPU v7x, 32 devices: a whole 2x2x4 slice. The times are simulated.
32 devices in a mesh: rows: 8 (over y, x, core), cols: 4 (over z).
Axes of the slice: x: 2, y: 2, z: 4, core: 2. Of those that a mesh axis runs over, the one named last changes fastest.
Arguments:
- grads: bfloat16 [9216, 8192], P(('rows', 'cols')), may hold values from -6 to 6
- tests: float32 [64, 8192], P(None, 'cols'), may hold values from -6 to 6
Outputs:
- solution: float32 [64, 8192], P(None, 'cols')
- scores: float32 [64, 9216], P(None, ('rows', 'cols'))
All inputs are finite; a program needn't handle non-finite values.
Results may differ from a plain program's by a relative error of at most 0.0041.
Values may be sent and summed in bfloat16 or wider, within the bound.
A program may use at most 64 MiB of HBM per device.

v0:
```python
import jax
import jax.numpy as jnp
from jax import lax
from jax.sharding import PartitionSpec as P

ITERS = 2
damping = 0.5


def per_device(grads, tests):
    n_rows = lax.axis_size("rows")
    n_cols = lax.axis_size("cols")
    n_total = grads.shape[0] * n_rows * n_cols
    width = grads.shape[1]
    solution = jnp.zeros(tests.shape, jnp.float32)
    residual = tests
    direction = tests
    norm_now = lax.psum(jnp.sum(residual * residual, axis=1), "cols")
    for step in range(ITERS):
        proj = lax.dot_general(
            grads,
            lax.all_gather(direction.astype(jnp.bfloat16), "cols", axis=1, tiled=True),
            (((1,), (1,)), ((), ())),
            preferred_element_type=jnp.float32,
        ).astype(jnp.bfloat16)
        partial_value = lax.dot_general(
            proj, grads, (((0,), (0,)), ((), ())), preferred_element_type=jnp.float32
        )
        owned = lax.psum_scatter(partial_value, "cols", scatter_dimension=1, tiled=True)
        owned = lax.psum(owned, "rows")
        image = owned / n_total + damping * direction
        curv, cross, image_sq = lax.psum(
            (
                jnp.sum(direction * image, axis=1),
                jnp.sum(residual * image, axis=1),
                jnp.sum(image * image, axis=1),
            ),
            "cols",
        )
        alpha = norm_now / curv
        norm_next = norm_now - 2.0 * alpha * cross + alpha * alpha * image_sq
        solution = solution + alpha[:, None] * direction
        residual = residual - alpha[:, None] * image
        if step + 1 < ITERS:
            direction = residual + (norm_next / norm_now)[:, None] * direction
            norm_now = norm_next
    scores = lax.dot_general(
        lax.all_gather(solution.astype(jnp.bfloat16), "cols", axis=1, tiled=True),
        grads,
        (((1,), (1,)), ((), ())),
        preferred_element_type=jnp.float32,
    )
    return (solution, scores * width ** (-0.5))


def solution(mesh):
    placed = (P(("rows", "cols"), None), P(None, "cols"))
    return jax.shard_map(
        per_device,
        mesh=mesh,
        in_specs=placed,
        out_specs=(P(None, "cols"), P(None, ("rows", "cols"))),
        check_vma=False,
    )
```

profile of v0, /device:TPU:0, one launch (start us, length us, event | category | flops | bytes accessed | tf_op | source)
XLA Modules:
  0.0 350.8 jit_solution(4595125535650454993)
XLA Ops:
  7.2 0.0 all-gather.4.cloned.1.call-start
  7.2 1.8 convert_element_type.16
  9.0 0.0 reduce-scatter.3.cloned.1.call-start
  9.1 31.8 %all-gather.4.cloned.1.call-done = bf16[64,8192]{1,0:T(8,128)(2,1)} async-done(((bf16[64,2048]{1,0:T(8,128)(2,1)}), bf16[64,8192]{1,0:T(8,128)(2,1)}) %all-gather.4.cloned.1.call-update) | async-done | bytes 1048592 | tf_op jit(solution)/shard_map/all_gather | solution.py:22
  40.9 9.4 %fusion = f32[64,8192]{1,0:T(8,128)} fusion(bf16[288,8192]{1,0:T(8,128)(2,1)} %param.2, bf16[64,8192]{1,0:T(8,128)(2,1)} %all-gather.4.cloned.1.call-done), kind=kOutput, calls=%fused_computation.2 | convolution fusion | flops 603998208 | bytes 7864320 | tf_op jit(solution)/shard_map/dot_general | solution.py:26
  50.3 0.0 all-reduce.4.cloned.1.call-start
  50.4 43.1 %reduce-scatter.3.cloned.1.call-done = f32[64,2048]{1,0:T(8,128)} async-done(((f32[64,8192]{1,0:T(8,128)}), f32[64,2048]{1,0:T(8,128)}) %reduce-scatter.3.cloned.1.call-update) | async-done | bytes 524304 | tf_op jit(solution)/shard_map/reduce_scatter | solution.py:29
  93.5 0.0 all-gather.6.cloned.1.call-start
  93.5 57.1 %all-reduce.4.cloned.1.call-done = f32[64,2048]{1,0:T(8,128)} async-done(((f32[64,2048]{1,0:T(8,128)}), f32[64,2048]{1,0:T(8,128)}) %all-reduce.4.cloned.1.call-update) | async-done | bytes 524304 | tf_op jit(solution)/shard_map/psum | solution.py:30
  150.6 1.3 multiply_reduce_fusion.2
  151.9 11.6 %all-reduce = (f32[64]{0:T(128)S(1)}, f32[64]{0:T(128)S(1)}, f32[64]{0:T(128)S(1)}) all-reduce(f32[64]{0:T(128)S(1)} %get-tuple-element.3, f32[64]{0:T(128)S(1)} %get-tuple-element.4, f32[64]{0:T(128)S(1)} %get-tuple-element.2), channel_id=1, replica_groups=mesh['rows'=8,'cols'=4] {'cols'}, use_global_device_ids=true, to_apply=%region_7.0 | all-reduce | flops 192 | bytes 1536 | tf_op jit(solution)/shard_map/psum | solution.py:32
  163.6 1.9 fusion.2
  165.5 0.0 reduce-scatter.5.cloned.1.call-start
  165.6 24.7 %all-gather.6.cloned.1.call-done = bf16[64,8192]{1,0:T(8,128)(2,1)} async-done(((bf16[64,2048]{1,0:T(8,128)(2,1)}), bf16[64,8192]{1,0:T(8,128)(2,1)}) %all-gather.6.cloned.1.call-update) | async-done | bytes 1048592 | tf_op jit(solution)/shard_map/all_gather | solution.py:22
  190.3 9.6 %fusion.1 = f32[64,8192]{1,0:T(8,128)} fusion(bf16[288,8192]{1,0:T(8,128)(2,1)} %param.2, bf16[64,8192]{1,0:T(8,128)(2,1)} %all-gather.6.cloned.1.call-done), kind=kOutput, calls=%fused_computation.4 | convolution fusion | flops 603998208 | bytes 7864320 | tf_op jit(solution)/shard_map/dot_general | solution.py:26
  199.9 0.0 all-reduce.6.cloned.1.call-start
  199.9 43.1 %reduce-scatter.5.cloned.1.call-done = f32[64,2048]{1,0:T(8,128)} async-done(((f32[64,8192]{1,0:T(8,128)}), f32[64,2048]{1,0:T(8,128)}) %reduce-scatter.5.cloned.1.call-update) | async-done | bytes 524304 | tf_op jit(solution)/shard_map/reduce_scatter | solution.py:29
  243.1 0.0 all-gather.8.cloned.1.call-start
  243.1 56.9 %all-reduce.6.cloned.1.call-done = f32[64,2048]{1,0:T(8,128)} async-done(((f32[64,2048]{1,0:T(8,128)}), f32[64,2048]{1,0:T(8,128)}) %all-reduce.6.cloned.1.call-update) | async-done | bytes 524304 | tf_op jit(solution)/shard_map/psum | solution.py:30
  300.1 1.4 multiply_reduce_fusion
  301.5 11.6 %psum.50 = f32[64]{0:T(128)S(1)} all-reduce(f32[64]{0:T(128)S(1)} %multiply_reduce_fusion), channel_id=1, replica_groups=mesh['rows'=8,'cols'=4] {'cols'}, use_global_device_ids=true, to_apply=%region_11.0 | all-reduce | flops 64 | bytes 512 | tf_op jit(solution)/shard_map/psum | solution.py:32
  313.1 1.1 fusion.3
  314.3 24.8 %all-gather.8.cloned.1.call-done = bf16[64,8192]{1,0:T(8,128)(2,1)} async-done(((bf16[64,2048]{1,0:T(8,128)(2,1)}), bf16[64,8192]{1,0:T(8,128)(2,1)}) %all-gather.8.cloned.1.call-update) | async-done | bytes 1048592 | tf_op jit(solution)/shard_map/all_gather | solution.py:48
  339.0 5.0 %convolution_multiply_fusion = f32[64,288]{1,0:T(8,128)} fusion(bf16[64,8192]{1,0:T(8,128)(2,1)} %all-gather.8.cloned.1.call-done, bf16[288,8192]{1,0:T(8,128)(2,1)} %param.2), kind=kOutput, calls=%fused_computation.1 | convolution fusion | flops 302008320 | bytes 5840896 | tf_op jit(solution)/shard_map/dot_general | solution.py:47
  (13 shorter events, 0.1 us)
Async XLA Ops:
  7.2 33.7 %all-gather.4.cloned.1.call-start = ((), (), s32[]{:S(2)}) async-start(), calls=%async_computation.2 | async-start | bytes 1310720 | tf_op jit(solution)/shard_map/all_gather | solution.py:22
  9.0 141.6 %copy-start = (f32[64,2048]{1,0:T(8,128)S(1)}, f32[64,2048]{1,0:T(8,128)}, u32[]{:S(2)}) copy-start(f32[64,2048]{1,0:T(8,128)} %param.3) | copy-start | bytes 1572868
  9.0 84.5 %reduce-scatter.3.cloned.1.call-start = ((), (), s32[]{:S(2)}) async-start(), calls=%async_computation.3 | async-start | bytes 2621440 | tf_op jit(solution)/shard_map/reduce_scatter | solution.py:29
  50.3 100.3 %all-reduce.4.cloned.1.call-start = ((), (), s32[]{:S(2)}) async-start(), calls=%async_computation.4 | async-start | bytes 1048576 | tf_op jit(solution)/shard_map/psum | solution.py:30
  93.5 96.8 %all-gather.6.cloned.1.call-start = ((), (), s32[]{:S(2)}) async-start(), calls=%async_computation.5 | async-start | bytes 1310720 | tf_op jit(solution)/shard_map/all_gather | solution.py:22
  165.5 134.5 %copy-start.1 = (f32[64,2048]{1,0:T(8,128)S(1)}, f32[64,2048]{1,0:T(8,128)}, u32[]{:S(2)}) copy-start(f32[64,2048]{1,0:T(8,128)} %all-reduce.4.cloned.1.call-done) | copy-start | bytes 1572868
  165.5 77.5 %reduce-scatter.5.cloned.1.call-start = ((), (), s32[]{:S(2)}) async-start(), calls=%async_computation.6 | async-start | bytes 2621440 | tf_op jit(solution)/shard_map/reduce_scatter | solution.py:29
  199.9 100.2 %all-reduce.6.cloned.1.call-start = ((), (), s32[]{:S(2)}) async-start(), calls=%async_computation.7 | async-start | bytes 1048576 | tf_op jit(solution)/shard_map/psum | solution.py:30
  243.1 95.9 %all-gather.8.cloned.1.call-start = ((), (), s32[]{:S(2)}) async-start(), calls=%async_computation.8 | async-start | bytes 1310720 | tf_op jit(solution)/shard_map/all_gather | solution.py:48
Sparse Core Ops, SparseCore 0:
  10.1 30.6 all-gather.3
  50.4 43.0 reduce-scatter.2
  96.6 53.9 all-reduce.3
  165.6 24.5 all-gather.5
  200.0 43.0 reduce-scatter.4
  246.0 53.9 all-reduce.5
  314.4 24.5 all-gather.7
where the time goes:
time: 351 us
  waiting for transfers between devices  282 us (80%)
  matrix products  24 us (7%)
  blocking collectives  23.2 us (7%)
  between operations  14.1 us (4%)
  other arithmetic  7.59 us (2%)
    psum x2, waiting for transfers between devices, per_device(): owned = lax.psum(owned, 'rows')  114 us
    reduce_scatter x2, waiting for transfers between devices, per_device(): lax.psum_scatter(partial_value, 'cols', scatter_dimension=1, tiled=True)  86.2 us
    all_gather x2, waiting for transfers between devices, per_device(): lax.all_gather(direction.astype(jnp.bfloat16), 'cols', axis=1, tiled=True)  56.5 us
    all_gather x1, waiting for transfers between devices, per_device(): lax.all_gather(solution.astype(jnp.bfloat16), 'cols', axis=1, tiled=True)  24.8 us
    psum x2, blocking collectives, per_device(): lax.psum((jnp.sum(direction * image, axis=1), jnp.sum(residual * image, a...  23.2 us
    dot_general x2, matrix products, per_device(): lax.dot_general(proj, grads, (((0,), (0,)), ((), ())), preferred_element_...  19 us
  transfers between devices with their start and end apart: 7, of which 7 were waited for; matrix products, arithmetic and copies ran while one was open for 0% of the time, Pallas kernels for 0%

commit v1 on v0

--- a/solution.py
+++ b/solution.py
@@ -5,6 +5,27 @@
 
 ITERS = 2
 damping = 0.5
+
+
+def ring_gather(x, axis, dim):
+    length, index, extent = (lax.axis_size(axis), lax.axis_index(axis), x.shape[dim])
+    upward = [(i, (i + 1) % length) for i in range(length)]
+    left = [(i, (i - 1) % length) for i in range(length)]
+    whole = jnp.zeros((*x.shape[:dim], length * extent, *x.shape[dim + 1 :]), x.dtype)
+    whole = lax.dynamic_update_slice_in_dim(whole, x, index * extent, axis=dim)
+    from_left = from_right = x
+    halfway = length // 2
+    for turn in range(1, halfway + 1):
+        from_left = lax.ppermute(from_left, axis, upward)
+        whole = lax.dynamic_update_slice_in_dim(
+            whole, from_left, (index - turn) % length * extent, axis=dim
+        )
+        if turn < length - halfway:
+            from_right = lax.ppermute(from_right, axis, left)
+            whole = lax.dynamic_update_slice_in_dim(
+                whole, from_right, (index + turn) % length * extent, axis=dim
+            )
+    return whole
 
 
 def per_device(grads, tests):
@@ -45,7 +66,7 @@
             direction = residual + (norm_next / norm_now)[:, None] * direction
             norm_now = norm_next
     scores = lax.dot_general(
-        lax.all_gather(solution.astype(jnp.bfloat16), "cols", axis=1, tiled=True),
+        ring_gather(solution.astype(jnp.bfloat16), "cols", 1),
         grads,
         (((1,), (1,)), ((), ())),
         preferred_element_type=jnp.float32,

time: 351 us -> 345 us (0.983)
  waiting for transfers between devices: 282 us -> 272 us
  starting transfers between devices: 0.28 us -> 4.07 us
    all_gather x1 -> x0, waiting for transfers between devices: 24.8 us -> none  [per_device(): lax.all_gather(solution.astype(jnp.bfloat16), 'cols', axis=1, tiled=True)]
    ppermute x0 -> x3, waiting for transfers between devices: none -> 15.4 us  [the longest x2 13.6 us: ring_gather(): from_left = lax.ppermute(from_left, axis, upward)]
    ppermute x0 -> x3, starting transfers between devices: none -> 3.83 us  [the longest x1 3.82 us: ring_gather(): from_right = lax.ppermute(from_right, axis, left)]
  transfers between devices with their start and end apart: 7 -> 9, of which waited for: 7 -> 9; matrix products, arithmetic and copies ran while one was open for 0% -> 0% of each run, Pallas kernels for 0% -> 0%
where the time goes in v1:
time: 345 us
  waiting for transfers between devices  272 us (79%)
  matrix products  23.6 us (7%)
  blocking collectives  23.2 us (7%)
  between operations  14.2 us (4%)
  other arithmetic  7.51 us (2%)
  starting transfers between devices  4.07 us (1%)
    psum x2, waiting for transfers between devices, per_device(): owned = lax.psum(owned, 'rows')  114 us
    reduce_scatter x2, waiting for transfers between devices, per_device(): lax.psum_scatter(partial_value, 'cols', scatter_dimension=1, tiled=True)  86.2 us
    all_gather x2, waiting for transfers between devices, per_device(): lax.all_gather(direction.astype(jnp.bfloat16), 'cols', axis=1, tiled=True)  56.5 us
    psum x2, blocking collectives, per_device(): lax.psum((jnp.sum(direction * image, axis=1), jnp.sum(residual * image, a...  23.2 us
    dot_general x2, matrix products, per_device(): lax.dot_general(proj, grads, (((0,), (0,)), ((), ())), preferred_element_...  19 us
    ppermute x2, waiting for transfers between devices, ring_gather(): from_left = lax.ppermute(from_left, axis, upward)  13.6 us
  transfers between devices with their start and end apart: 9, of which 9 were waited for; matrix products, arithmetic and copies ran while one was open for 0% of the time, Pallas kernels for 0%

profile of v1, /device:TPU:0, one launch (start us, length us, event | category | flops | bytes accessed | tf_op | source)
XLA Modules:
  0.0 345.0 jit_solution(13614083318537908008)
XLA Ops:
  7.2 1.8 convert_element_type.16
  9.0 0.0 reduce-scatter.3.cloned.1.call-start
  9.1 31.8 %all-gather.3.cloned.1.call-done = bf16[64,8192]{1,0:T(8,128)(2,1)} async-done(((bf16[64,2048]{1,0:T(8,128)(2,1)}), bf16[64,8192]{1,0:T(8,128)(2,1)}) %all-gather.3.cloned.1.call-update) | async-done | bytes 1048592 | tf_op jit(solution)/shard_map/all_gather | solution.py:43
  40.9 9.4 %fusion = f32[64,8192]{1,0:T(8,128)} fusion(bf16[288,8192]{1,0:T(8,128)(2,1)} %param.2, bf16[64,8192]{1,0:T(8,128)(2,1)} %all-gather.3.cloned.1.call-done), kind=kOutput, calls=%fused_computation.2 | convolution fusion | flops 603998208 | bytes 7864320 | tf_op jit(solution)/shard_map/dot_general | solution.py:47
  50.4 43.1 %reduce-scatter.3.cloned.1.call-done = f32[64,2048]{1,0:T(8,128)} async-done(((f32[64,8192]{1,0:T(8,128)}), f32[64,2048]{1,0:T(8,128)}) %reduce-scatter.3.cloned.1.call-update) | async-done | bytes 524304 | tf_op jit(solution)/shard_map/reduce_scatter | solution.py:50
  93.5 57.1 %all-reduce.4.cloned.1.call-done = f32[64,2048]{1,0:T(8,128)} async-done(((f32[64,2048]{1,0:T(8,128)}), f32[64,2048]{1,0:T(8,128)}) %all-reduce.4.cloned.1.call-update) | async-done | bytes 524304 | tf_op jit(solution)/shard_map/psum | solution.py:51
  150.6 1.3 multiply_reduce_fusion.2
  151.9 11.6 %all-reduce = (f32[64]{0:T(128)S(1)}, f32[64]{0:T(128)S(1)}, f32[64]{0:T(128)S(1)}) all-reduce(f32[64]{0:T(128)S(1)} %get-tuple-element.3, f32[64]{0:T(128)S(1)} %get-tuple-element.4, f32[64]{0:T(128)S(1)} %get-tuple-element.2), channel_id=1, replica_groups=mesh['rows'=8,'cols'=4] {'cols'}, use_global_device_ids=true, to_apply=%region_7.0 | all-reduce | flops 192 | bytes 1536 | tf_op jit(solution)/shard_map/psum | solution.py:53
  163.6 1.9 fusion.2
  165.5 0.0 reduce-scatter.5.cloned.1.call-start
  165.6 24.7 %all-gather.5.cloned.1.call-done = bf16[64,8192]{1,0:T(8,128)(2,1)} async-done(((bf16[64,2048]{1,0:T(8,128)(2,1)}), bf16[64,8192]{1,0:T(8,128)(2,1)}) %all-gather.5.cloned.1.call-update) | async-done | bytes 1048592 | tf_op jit(solution)/shard_map/all_gather | solution.py:43
  190.3 9.6 %fusion.1 = f32[64,8192]{1,0:T(8,128)} fusion(bf16[288,8192]{1,0:T(8,128)(2,1)} %param.2, bf16[64,8192]{1,0:T(8,128)(2,1)} %all-gather.5.cloned.1.call-done), kind=kOutput, calls=%fused_computation.4 | convolution fusion | flops 603998208 | bytes 7864320 | tf_op jit(solution)/shard_map/dot_general | solution.py:47
  199.9 0.0 all-reduce.6.cloned.1.call-start
  199.9 43.1 %reduce-scatter.5.cloned.1.call-done = f32[64,2048]{1,0:T(8,128)} async-done(((f32[64,8192]{1,0:T(8,128)}), f32[64,2048]{1,0:T(8,128)}) %reduce-scatter.5.cloned.1.call-update) | async-done | bytes 524304 | tf_op jit(solution)/shard_map/reduce_scatter | solution.py:50
  243.1 57.0 %all-reduce.6.cloned.1.call-done = f32[64,2048]{1,0:T(8,128)} async-done(((f32[64,2048]{1,0:T(8,128)}), f32[64,2048]{1,0:T(8,128)}) %all-reduce.6.cloned.1.call-update) | async-done | bytes 524304 | tf_op jit(solution)/shard_map/psum | solution.py:51
  300.1 1.4 multiply_reduce_fusion
  301.5 11.6 %psum.50 = f32[64]{0:T(128)S(1)} all-reduce(f32[64]{0:T(128)S(1)} %multiply_reduce_fusion), channel_id=1, replica_groups=mesh['rows'=8,'cols'=4] {'cols'}, use_global_device_ids=true, to_apply=%region_11.0 | all-reduce | flops 64 | bytes 512 | tf_op jit(solution)/shard_map/psum | solution.py:53
  313.1 0.1 broadcast_in_dim.2
  313.2 1.1 constant_dynamic-update-slice_fusion.3
  314.2 3.8 %collective-permute-start.1 = (bf16[64,2048]{1,0:T(8,128)(2,1)S(1)}, bf16[64,2048]{1,0:T(8,128)(2,1)S(1)}, u32[]{:S(2)}, u32[]{:S(2)}) collective-permute-start(bf16[64,2048]{1,0:T(8,128)(2,1)S(1)} %get-tuple-element.9), channel_id=1, source_target_pairs={{0,3},{1,0},{2,1},{3,2},{4,7},{5,4},{6,5},{7,6},{8,11},{9,8},{10,9... | collective-permute-start | bytes 786440 | tf_op jit(solution)/shard_map/ppermute | solution.py:24
  318.1 7.3 %collective-permute-done = bf16[64,2048]{1,0:T(8,128)(2,1)S(1)} collective-permute-done((bf16[64,2048]{1,0:T(8,128)(2,1)S(1)}, bf16[64,2048]{1,0:T(8,128)(2,1)S(1)}, u32[]{:S(2)}, u32[]{:S(2)}) %collective-permute-start) | collective-permute-done | bytes 262176 | tf_op jit(solution)/shard_map/ppermute | solution.py:19
  325.3 1.8 collective-permute-done.1
  327.1 6.4 %collective-permute-done.2 = bf16[64,2048]{1,0:T(8,128)(2,1)S(1)} collective-permute-done((bf16[64,2048]{1,0:T(8,128)(2,1)S(1)}, bf16[64,2048]{1,0:T(8,128)(2,1)S(1)}, u32[]{:S(2)}, u32[]{:S(2)}) %collective-permute-start.2) | collective-permute-done | bytes 262176 | tf_op jit(solution)/shard_map/ppermute | solution.py:19
  333.5 4.6 %convolution_multiply_fusion = f32[64,288]{1,0:T(8,128)} fusion(bf16[64,8192]{1,0:T(8,128)(2,1)S(1)} %constant_dynamic-update-slice_fusion, bf16[288,8192]{1,0:T(8,128)(2,1)} %param.2), kind=kOutput, calls=%fused_computation.1 | convolution fusion | flops 302008320 | bytes 5840896 | tf_op jit(solution)/shard_map/dot_general | solution.py:68
  (20 shorter events, 0.3 us)
Async XLA Ops:
  7.2 33.7 %all-gather.3.cloned.1.call-start = ((), (), s32[]{:S(2)}) async-start(), calls=%async_computation.2 | async-start | bytes 1310720 | tf_op jit(solution)/shard_map/all_gather | solution.py:43
  9.0 141.6 %copy-start = (f32[64,2048]{1,0:T(8,128)S(1)}, f32[64,2048]{1,0:T(8,128)}, u32[]{:S(2)}) copy-start(f32[64,2048]{1,0:T(8,128)} %param.3) | copy-start | bytes 1572868
  9.0 84.5 %reduce-scatter.3.cloned.1.call-start = ((), (), s32[]{:S(2)}) async-start(), calls=%async_computation.3 | async-start | bytes 2621440 | tf_op jit(solution)/shard_map/reduce_scatter | solution.py:50
  50.3 100.3 %all-reduce.4.cloned.1.call-start = ((), (), s32[]{:S(2)}) async-start(), calls=%async_computation.4 | async-start | bytes 1048576 | tf_op jit(solution)/shard_map/psum | solution.py:51
  93.5 96.8 %all-gather.5.cloned.1.call-start = ((), (), s32[]{:S(2)}) async-start(), calls=%async_computation.5 | async-start | bytes 1310720 | tf_op jit(solution)/shard_map/all_gather | solution.py:43
  165.5 134.5 %copy-start.1 = (f32[64,2048]{1,0:T(8,128)S(1)}, f32[64,2048]{1,0:T(8,128)}, u32[]{:S(2)}) copy-start(f32[64,2048]{1,0:T(8,128)} %all-reduce.4.cloned.1.call-done) | copy-start | bytes 1572868
  165.5 77.5 %reduce-scatter.5.cloned.1.call-start = ((), (), s32[]{:S(2)}) async-start(), calls=%async_computation.6 | async-start | bytes 2621440 | tf_op jit(solution)/shard_map/reduce_scatter | solution.py:50
  199.9 100.2 %all-reduce.6.cloned.1.call-start = ((), (), s32[]{:S(2)}) async-start(), calls=%async_computation.7 | async-start | bytes 1048576 | tf_op jit(solution)/shard_map/psum | solution.py:51
  314.2 11.1 %collective-permute-start = (bf16[64,2048]{1,0:T(8,128)(2,1)S(1)}, bf16[64,2048]{1,0:T(8,128)(2,1)S(1)}, u32[]{:S(2)}, u32[]{:S(2)}) collective-permute-start(bf16[64,2048]{1,0:T(8,128)(2,1)S(1)} %get-tuple-element.9), channel_id=1, source_target_pairs={{0,1},{1,2},{2,3},{3,0},{4,5},{5,6},{6,7},{7,4},{8,9},{9,10},{10,1... | collective-permute-start | bytes 786440 | tf_op jit(solution)/shard_map/ppermute | solution.py:19
  314.2 12.9 %collective-permute-start.1 = (bf16[64,2048]{1,0:T(8,128)(2,1)S(1)}, bf16[64,2048]{1,0:T(8,128)(2,1)S(1)}, u32[]{:S(2)}, u32[]{:S(2)}) collective-permute-start(bf16[64,2048]{1,0:T(8,128)(2,1)S(1)} %get-tuple-element.9), channel_id=1, source_target_pairs={{0,3},{1,0},{2,1},{3,2},{4,7},{5,4},{6,5},{7,6},{8,11},{9,8},{10,9... | collective-permute-start | bytes 786440 | tf_op jit(solution)/shard_map/ppermute | solution.py:24
  325.3 8.2 %collective-permute-start.2 = (bf16[64,2048]{1,0:T(8,128)(2,1)S(1)}, bf16[64,2048]{1,0:T(8,128)(2,1)S(1)}, u32[]{:S(2)}, u32[]{:S(2)}) collective-permute-start(bf16[64,2048]{1,0:T(8,128)(2,1)S(1)} %collective-permute-done), channel_id=1, source_target_pairs={{0,1},{1,2},{2,3},{3,0},{4,5},{5,6},{6,7},{7,4},{8,9},{9,10},{10,1... | collective-permute-start | bytes 786440 | tf_op jit(solution)/shard_map/ppermute | solution.py:19
Sparse Core Ops, SparseCore 0:
  10.1 30.6 all-gather.2
  50.4 43.0 reduce-scatter.2
  96.6 53.9 all-reduce.3
  165.6 24.5 all-gather.4
  200.0 43.0 reduce-scatter.4
  246.0 53.9 all-reduce.5
